TPU v7x, 512 devices: a whole 4x8x8 slice. The times are simulated.
512 devices in a mesh: grp: 4 (over y_lo, core), src: 16 (over y_hi, x), rcv: 8 (over z).
Axes of the slice: x: 4, y: 8 (y_hi: 4, y_lo: 2; y = y_hi * 2 + y_lo), z: 8, core: 2. Of those that a mesh axis runs over, the one named last changes fastest.
Arguments:
- recorded: bfloat16 [4, 2, 4096, 4096], P('grp', None, 'src', 'rcv'), parts along dimension 0, as said below
- aperture: int32 [128, 32, 3], P(('grp', 'src'), 'rcv'), parts along dimension 0, may hold values from 0 to 32, as said below
Outputs:
- multiples: float32 [4, 2, 4096, 4096], P('grp', None, 'src', 'rcv'), parts along dimension 0
There are 4 independent parts, one for each index of `grp`. A program takes and returns all parts, laid end to end along the dimension named above; each array names one. Nothing has to cross between parts.
Inputs may be any that keep to these rules, and one draw needn't show every extreme that they name: The data obey reciprocity: recorded(f, c, q, j) equals recorded(f, c, j, q). `aperture`: field 1 is from 4 to 32, field 0 plus field 1 is at most 32, field 2 is from 0 to 2. In every draw some tile pair spans all 32 k-blocks and some has taper width 2.
All inputs are finite; a program needn't handle non-finite values.
Results may differ from a plain program's by a relative error of at most 0.0004.
Values may be sent and summed in bfloat16 or wider, within the bound.
No kernel may reach another device: no remote copies, remote signals or barrier semaphores. Data moves between devices by JAX's collectives and lax.ppermute only.
A program may use at most 64 MiB of HBM per device.

v0:
```python
import jax
import jax.numpy as jnp
from jax import lax
from jax.sharding import PartitionSpec as P

NB = 32
TILE = 128


def tile_weights(aperture):
    block_ids = jnp.arange(NB, dtype=jnp.int32)
    offset = block_ids[None, None, :] - aperture[..., 0:1]
    extent = aperture[..., 1:2]
    taper_width = aperture[..., 2:3]
    margin = jnp.minimum(offset, extent - 1 - offset)
    ramped = jnp.minimum(
        1.0, (margin + 1).astype(jnp.float32) / (taper_width + 1).astype(jnp.float32)
    )
    return jnp.where((offset >= 0) & (offset < extent), ramped, 0.0)


def shards(recorded, aperture):
    slices = recorded.shape[0]
    own_rows = recorded.shape[2]
    own_cols = recorded.shape[3]
    row_tiles = own_rows // TILE
    col_tiles = own_cols // TILE
    weights = tile_weights(aperture)
    block_ids = jnp.arange(NB, dtype=jnp.int32)
    left_panel = lax.all_gather(recorded, "rcv", axis=3, tiled=True)

    def block_terms(incoming, first_row, span_rows, tile_weight):
        part_left = lax.dynamic_slice_in_dim(left_panel, first_row, span_rows, 3)
        part_left = part_left.reshape(slices, 2, row_tiles, TILE, span_rows)
        block_of = (first_row + jnp.arange(span_rows, dtype=jnp.int32)) // TILE
        row_weights = jnp.sum(
            jnp.where(block_of[:, None] == block_ids[None, :], tile_weight[:, :, None, :], 0.0),
            axis=-1,
        )
        scaled = (part_left[:, :, :, None, :, :] * row_weights[None, None, :, :, None, :]).astype(
            jnp.bfloat16
        )
        sub_tiles = tile_weight.shape[1]
        right_tiles = incoming.reshape(slices, 2, span_rows, sub_tiles, TILE)
        products = jnp.einsum(
            "fastik,fbktj->fabstij", scaled, right_tiles, preferred_element_type=jnp.float32
        )
        return jnp.stack(
            [products[:, 0, 0] - products[:, 1, 1], products[:, 0, 1] + products[:, 1, 0]], 1
        )

    empty = jnp.zeros((slices, 2, row_tiles, col_tiles, TILE, TILE), jnp.float32)
    incoming = lax.all_gather(recorded, "src", axis=2, tiled=True)
    extent = incoming.shape[2]

    def add_block(first_row, span_rows, running):
        portion = lax.dynamic_slice_in_dim(incoming, first_row, span_rows, 2)
        return running + block_terms(portion, first_row, span_rows, weights)

    sweeps = extent // TILE
    summed = lax.fori_loop(
        0, sweeps, lambda number, running: add_block(number * TILE, TILE, running), empty
    )
    return summed.transpose(0, 1, 2, 4, 3, 5).reshape(slices, 2, own_rows, own_cols)


def solution(mesh):
    in_specs = (P("grp", None, "src", "rcv"), P(("grp", "src"), "rcv", None))
    out_specs = P("grp", None, "src", "rcv")
    return jax.shard_map(shards, mesh=mesh, in_specs=in_specs, out_specs=out_specs, check_vma=False)
```

profile of v0, /device:TPU:1, one launch (start us, length us, event | category | flops | bytes accessed | tf_op | source)
XLA Modules:
  0.0 312.6 jit_solution(3568070417147690657)
XLA Ops:
  7.3 2.0 copy.15
  10.1 63.1 %all-gather.5.cloned.1.call-done = bf16[1,2,256,4096]{3,2,1,0:T(8,128)(2,1)} async-done(((bf16[1,2,256,512]{3,2,1,0:T(8,128)(2,1)}), bf16[1,2,256,4096]{3,2,1,0:T(8,128)(2,1)}) %all-gather.5.cloned.1.call-update) | async-done | bytes 4194320 | tf_op jit(solution)/shard_map/all_gather | solution.py:30
  73.2 131.2 %all-gather.3.cloned.1.call-done = bf16[1,2,4096,512]{2,3,1,0:T(8,128)(2,1)} async-done(((bf16[1,2,256,512]{2,3,1,0:T(8,128)(2,1)}), bf16[1,2,4096,512]{2,3,1,0:T(8,128)(2,1)}) %all-gather.3.cloned.1.call-update) | async-done | bytes 8388624 | tf_op jit(solution)/shard_map/all_gather | solution.py:53
  204.4 99.5 %while.16 = (s32[]{:T(128)}, f32[1,2,2,4,128,128]{4,5,2,3,1,0:T(8,128)S(1)}, bf16[1,2,4096,512]{2,3,1,0:T(8,128)(2,1)}, bf16[1,2,256,4096]{3,2,1,0:T(8,128)(2,1)...) while((s32[]{:T(128)}, ...), condition=%wide.region_2.3_spmd.clone, body=%wide.region_0.2_spmd.clone.sunk | while | flops 135929600 | bytes 10120505 | solution.py:61
  205.4 1.0 constant_dynamic-slice_fusion.5
  208.5 1.0 constant_dynamic-slice_fusion.5
  211.6 1.0 constant_dynamic-slice_fusion.5
  214.7 1.0 constant_dynamic-slice_fusion.5
  217.8 1.0 constant_dynamic-slice_fusion.5
  220.9 1.0 constant_dynamic-slice_fusion.5
  224.0 1.0 constant_dynamic-slice_fusion.5
  227.1 1.0 constant_dynamic-slice_fusion.5
  230.2 1.0 constant_dynamic-slice_fusion.5
  233.4 1.0 constant_dynamic-slice_fusion.5
  236.5 1.0 constant_dynamic-slice_fusion.5
  239.6 1.0 constant_dynamic-slice_fusion.5
  242.7 1.0 constant_dynamic-slice_fusion.5
  245.8 1.0 constant_dynamic-slice_fusion.5
  248.9 1.0 constant_dynamic-slice_fusion.5
  252.0 1.0 constant_dynamic-slice_fusion.5
  255.1 1.0 constant_dynamic-slice_fusion.5
  258.3 1.0 constant_dynamic-slice_fusion.5
  267.6 1.0 constant_dynamic-slice_fusion.5
  273.8 1.0 constant_dynamic-slice_fusion.5
  276.9 1.0 constant_dynamic-slice_fusion.5
  280.0 1.0 constant_dynamic-slice_fusion.5
  283.1 1.0 constant_dynamic-slice_fusion.5
  286.3 1.0 constant_dynamic-slice_fusion.5
  289.4 1.0 constant_dynamic-slice_fusion.5
  295.6 1.0 constant_dynamic-slice_fusion.5
  301.8 1.0 constant_dynamic-slice_fusion.5
  304.4 1.4 reshape.136
  (364 shorter events, 72.1 us)
Async XLA Ops:
  6.5 66.7 %all-gather.5.cloned.1.call-start = ((), (), s32[]{:S(2)}) async-start(), calls=%async_computation.1 | async-start | bytes 4718592 | tf_op jit(solution)/shard_map/all_gather | solution.py:30
  7.3 197.1 %all-gather.3.cloned.1.call-start = ((), (), s32[]{:S(2)}) async-start(), calls=%async_computation | async-start | bytes 8912896 | tf_op jit(solution)/shard_map/all_gather | solution.py:53
Sparse Core Ops, SparseCore 0:
  9.4 63.7 all-gather.4
  76.2 128.1 all-gather.2
where the time goes:
time: 314 us; the launch traced here: 313 us
  waiting for transfers between devices  195 us (62%)
  local copies, waits for them, and re-layouts  64.6 us (21%)
  other arithmetic  22.6 us (7%)
  matrix products  13.9 us (4%)
  between operations  13.4 us (4%)
    all_gather x1, waiting for transfers between devices, shards(): incoming = lax.all_gather(recorded, 'src', axis=2, tiled=True)  131 us
    all_gather x1, waiting for transfers between devices, shards(): left_panel = lax.all_gather(recorded, 'rcv', axis=3, tiled=True)  63.1 us
    dynamic_slice x32, local copies, waits for them, and re-layouts, add_block(): portion = lax.dynamic_slice_in_dim(incoming, first_row, span_rows, 2)  31.2 us
    dynamic_slice x32, local copies, waits for them, and re-layouts, block_terms(): part_left = lax.dynamic_slice_in_dim(left_panel, first_row, span_rows, 3)  29.4 us
    dot_general x32, matrix products, block_terms(): jnp.einsum('fastik,fbktj->fabstij', scaled, right_tiles, preferred_elemen...  13.9 us
    add x32, other arithmetic, add_block(): return running + block_terms(portion, first_row, span_rows, weights)  10.7 us
  transfers between devices with their start and end apart: 2, of which 2 were waited for; matrix products, arithmetic and copies ran while one was open for 1% of the time, Pallas kernels for 0%

commit v1 on v0

--- a/solution.py
+++ b/solution.py
@@ -5,6 +5,11 @@
 
 NB = 32
 TILE = 128
+
+
+def gather_by_exchange(x, axis, dim):
+    copies = jnp.concatenate([x] * lax.axis_size(axis), axis=dim)
+    return lax.all_to_all(copies, axis, dim, dim, tiled=True)
 
 
 def tile_weights(aperture):
@@ -27,7 +32,7 @@
     col_tiles = own_cols // TILE
     weights = tile_weights(aperture)
     block_ids = jnp.arange(NB, dtype=jnp.int32)
-    left_panel = lax.all_gather(recorded, "rcv", axis=3, tiled=True)
+    left_panel = gather_by_exchange(recorded, "rcv", 3)
 
     def block_terms(incoming, first_row, span_rows, tile_weight):
         part_left = lax.dynamic_slice_in_dim(left_panel, first_row, span_rows, 3)

time: 314 us -> 263 us (0.84)
  waiting for transfers between devices: 195 us -> 116 us
  local copies, waits for them, and re-layouts: 64.6 us -> 82.3 us
  starting transfers between devices: 0.04 us -> 11 us
    all_gather x1, waiting for transfers between devices: 131 us -> 18.9 us  [shards(): incoming = lax.all_gather(recorded, 'src', axis=2, tiled=True)]
    all_to_all x0 -> x1, waiting for transfers between devices: none -> 96.8 us  [gather_by_exchange(): return lax.all_to_all(copies, axis, dim, dim, tiled=True)]
    all_gather x1 -> x0, waiting for transfers between devices: 63.1 us -> none  [shards(): left_panel = lax.all_gather(recorded, 'rcv', axis=3, tiled=True)]
    all_to_all x0 -> x1, starting transfers between devices: none -> 11 us  [gather_by_exchange(): return lax.all_to_all(copies, axis, dim, dim, tiled=True)]
    unnamed x1 -> x11, local copies, waits for them, and re-layouts: 2.04 us -> 11.5 us
    dynamic_slice x32 -> x64, local copies, waits for them, and re-layouts: 29.4 us -> 36.4 us  [block_terms(): part_left = lax.dynamic_slice_in_dim(left_panel, first_row, span_rows, 3)]
  transfers between devices with their start and end apart: 2 -> 2, of which waited for: 2 -> 2; matrix products, arithmetic and copies ran while one was open for 1% -> 4% of each run, Pallas kernels for 0% -> 0%
where the time goes in v1:
time: 263 us; the launch traced here: 261 us
  waiting for transfers between devices  116 us (44%)
  local copies, waits for them, and re-layouts  82.3 us (31%)
  other arithmetic  21.9 us (8%)
  matrix products  13.9 us (5%)
  between operations  13.4 us (5%)
  starting transfers between devices  11 us (4%)
  loops' own time  3.12 us (1%)
    all_to_all x1, waiting for transfers between devices, gather_by_exchange(): return lax.all_to_all(copies, axis, dim, dim, tiled=True)  96.8 us
    dynamic_slice x64, local copies, waits for them, and re-layouts, block_terms(): part_left = lax.dynamic_slice_in_dim(left_panel, first_row, span_rows, 3)  36.4 us
    dynamic_slice x32, local copies, waits for them, and re-layouts, add_block(): portion = lax.dynamic_slice_in_dim(incoming, first_row, span_rows, 2)  31.2 us
    all_gather x1, waiting for transfers between devices, shards(): incoming = lax.all_gather(recorded, 'src', axis=2, tiled=True)  18.9 us
    dot_general x32, matrix products, block_terms(): jnp.einsum('fastik,fbktj->fabstij', scaled, right_tiles, preferred_elemen...  13.9 us
    unnamed x11, local copies, waits for them, and re-layouts  11.5 us
    all_to_all x1, starting transfers between devices, gather_by_exchange(): return lax.all_to_all(copies, axis, dim, dim, tiled=True)  11 us
    add x32, other arithmetic, add_block(): return running + block_terms(portion, first_row, span_rows, weights)  10.7 us
  transfers between devices with their start and end apart: 2, of which 2 were waited for; matrix products, arithmetic and copies ran while one was open for 4% of the time, Pallas kernels for 0%

profile of v1, /device:TPU:1, one launch (start us, length us, event | category | flops | bytes accessed | tf_op | source)
XLA Modules:
  0.0 261.4 jit_solution(6966141159085065373)
XLA Ops:
  6.5 2.0 copy.29
  8.6 1.4 copy.30
  10.0 1.2 constant_dynamic-update-slice_fusion.7
  11.1 1.2 constant_dynamic-update-slice_fusion.6
  12.3 1.1 constant_dynamic-update-slice_fusion.5
  13.5 1.1 constant_dynamic-update-slice_fusion.4
  14.6 1.2 constant_dynamic-update-slice_fusion.3
  15.8 1.2 constant_dynamic-update-slice_fusion.2
  17.0 1.1 constant_dynamic-update-slice_fusion.1
  18.1 1.2 constant_dynamic-update-slice_fusion
  19.3 11.0 %all-to-all-start = ((bf16[1,2,256,4096]{2,1,0,3:T(2,128)(2,1)}), bf16[1,2,256,4096]{2,1,0,3:T(2,128)(2,1)}, u32[]{:S(2)}, u32[]{:S(2)}) async-start(bf16[1,2,256,4096]{2,1,0,3:T(2,128)(2,1)} %constant_dynamic-update-slice_fusion), calls=%async_computation | async-start | bytes 8388608 | tf_op jit(solution)/shard_map/all_to_all | solution.py:12
  30.3 96.8 %all-to-all-done = bf16[1,2,256,4096]{2,1,0,3:T(2,128)(2,1)} async-done(((bf16[1,2,256,4096]{2,1,0,3:T(2,128)(2,1)}), bf16[1,2,256,4096]{2,1,0,3:T(2,128)(2,1)}, u32[]{:S(2)}, u32[]{:S(2)}) %all-to-all-start) | async-done | bytes 4194336 | tf_op jit(solution)/shard_map/all_to_all | solution.py:12
  127.1 18.9 %all-gather.2.cloned.1.call-done = bf16[1,2,4096,512]{2,3,1,0:T(8,128)(2,1)} async-done(((bf16[1,2,256,512]{2,3,1,0:T(8,128)(2,1)}), bf16[1,2,4096,512]{2,3,1,0:T(8,128)(2,1)}) %all-gather.2.cloned.1.call-update) | async-done | bytes 8388624 | tf_op jit(solution)/shard_map/all_gather | solution.py:58
  146.0 106.7 %while.16 = (s32[]{:T(128)}, f32[1,2,2,4,128,128]{4,5,2,3,1,0:T(8,128)S(1)}, bf16[1,2,4096,512]{2,3,1,0:T(8,128)(2,1)}, bf16[1,2,256,4096]{2,1,0,3:T(2,128)(2,1)...) while((s32[]{:T(128)}, ...), condition=%wide.region_2.3_spmd.clone, body=%wide.region_0.2_spmd.clone.sunk | while | flops 135929600 | bytes 10382649 | solution.py:66
  149.3 1.0 constant_dynamic-slice_fusion.4
  152.6 1.0 constant_dynamic-slice_fusion.4
  156.0 1.0 constant_dynamic-slice_fusion.4
  159.3 1.0 constant_dynamic-slice_fusion.4
  162.6 1.0 constant_dynamic-slice_fusion.4
  166.0 1.0 constant_dynamic-slice_fusion.4
  169.3 1.0 constant_dynamic-slice_fusion.4
  172.6 1.0 constant_dynamic-slice_fusion.4
  189.3 1.0 constant_dynamic-slice_fusion.4
  199.3 1.0 constant_dynamic-slice_fusion.4
  209.3 1.0 constant_dynamic-slice_fusion.4
  216.0 1.0 constant_dynamic-slice_fusion.4
  219.4 1.0 constant_dynamic-slice_fusion.4
  226.0 1.0 constant_dynamic-slice_fusion.4
  236.0 1.0 constant_dynamic-slice_fusion.4
  239.4 1.0 constant_dynamic-slice_fusion.4
  246.0 1.0 constant_dynamic-slice_fusion.4
  253.1 1.4 reshape.136
  (406 shorter events, 87.0 us)
Async XLA Ops:
  6.5 139.4 %all-gather.2.cloned.1.call-start = ((), (), s32[]{:S(2)}) async-start(), calls=%async_computation.1 | async-start | bytes 8912896 | tf_op jit(solution)/shard_map/all_gather | solution.py:58
  19.3 11.0 %copy-start = (s32[2,4,3]{1,0,2:T(2,128)S(1)}, s32[2,4,3]{1,0,2:T(2,128)}, u32[]{:S(2)}) copy-start(s32[2,4,3]{1,0,2:T(2,128)} %param.5) | copy-start | bytes 292
  19.3 107.8 %all-to-all-start = ((bf16[1,2,256,4096]{2,1,0,3:T(2,128)(2,1)}), bf16[1,2,256,4096]{2,1,0,3:T(2,128)(2,1)}, u32[]{:S(2)}, u32[]{:S(2)}) async-start(bf16[1,2,256,4096]{2,1,0,3:T(2,128)(2,1)} %constant_dynamic-update-slice_fusion), calls=%async_computation | async-start | bytes 8388608 | tf_op jit(solution)/shard_map/all_to_all | solution.py:12
Sparse Core Ops, SparseCore 0:
  10.3 135.5 all-gather.1
